TPU v7x, 128 devices: a whole 4x4x4 slice. The times are simulated.
128 devices in a mesh: frame: 4 (over x), pix: 32 (over y, z, core).
Axes of the slice: x: 4, y: 4, z: 4, core: 2. Of those that a mesh axis runs over, the one named last changes fastest.
Arguments:
- frames: bfloat16 [128, 4, 512, 512], P('frame', None, 'pix'), may hold values from -26 to 26
- prev_fg: bfloat16 [128, 4, 512, 512], P('frame', None, 'pix'), may hold values from -3 to 3
- depth_valid: int32 [128, 512, 512], P('frame', 'pix'), may hold values 0 or 1
- sketch: float32 [128, 64], replicated, may hold values from -0.5 to 0.5
- tv_weight: float32 [4], replicated, may hold values from 0.1 to 1
Outputs:
- background: bfloat16 [128, 4, 512, 512], P('frame', None, 'pix')
- foreground: bfloat16 [128, 4, 512, 512], P('frame', None, 'pix')
All inputs are finite; a program needn't handle non-finite values. No bound on the sum of `depth_valid` on one device may be relied on, other than what follows from the above.
Results may differ from a plain program's by a relative error of at most 0.012.
The roundings to bfloat16 on the way count: a program that leaves them out, or rounds other values in their place, can miss the bound.
Values may be sent and summed in bfloat16 or wider, within the bound.
A program may use at most 64 MiB of HBM per device.

v0:
```python
import jax
import jax.numpy as jnp
from jax import lax
from jax.sharding import PartitionSpec as P

POWER = 3
NSWEEP = 5
STEP_SIZE = 0.125


def shortened(shard):

    def short(part):
        return part.astype(jnp.bfloat16) if part.dtype == jnp.float32 else part

    return jax.tree.map(short, shard)


def from_behind(value, axis, steps):
    count = lax.axis_size(axis)
    leading, last = (max(0, -steps), min(count, count - steps))
    return lax.ppermute(value, axis, [(source, source + steps) for source in range(leading, last)])


def exact_dot(left, right):
    return jnp.dot(left, right, precision=lax.Precision.HIGHEST)


def mixing_matrix(gram, sketch):
    basis = sketch
    for turn in range(POWER):
        image = exact_dot(gram, basis)
        factor = jnp.linalg.cholesky(exact_dot(basis.T, image))
        basis = lax.linalg.triangular_solve(
            factor, image, left_side=False, lower=True, transpose_a=True
        )
    image = exact_dot(gram, basis)
    factor = jnp.linalg.cholesky(exact_dot(basis.T, image))
    middle = lax.linalg.triangular_solve(
        factor, exact_dot(basis.T, gram), left_side=True, lower=True
    )
    coeffs = lax.linalg.triangular_solve(
        factor, middle, left_side=True, lower=True, transpose_a=True
    )
    return exact_dot(basis, coeffs)


def pair_rows(left, right):
    return lax.dot_general(
        left, right, (((1,), (1,)), ((), ())), preferred_element_type=jnp.float32
    )


def over_frames(weights, pixels):
    return lax.dot_general(
        weights, pixels, (((0,), (0,)), ((), ())), preferred_element_type=jnp.float32
    )


def dual_update(first, second, down, across, step):
    size = jnp.sqrt(down * down + across * across)
    scale = 1.0 + step * size
    return ((first - step * down) / scale, (second - step * across) / scale)


def col_prev(field):
    return jnp.pad(field[:, :, :, :-1], ((0, 0), (0, 0), (0, 0), (1, 0)))


def col_grad(smooth, last_col):
    next_cols = jnp.pad(smooth[:, :, :, 1:], ((0, 0), (0, 0), (0, 0), (0, 1)))
    return jnp.where(last_col, 0.0, next_cols - smooth)


def local(frames, prev_fg, depth_valid, sketch, tv_weight):
    count, chans, rows, cols = frames.shape
    height = rows * lax.axis_size("pix")
    nval = chans * height * cols
    start_frame = lax.axis_index("frame") * count
    chan_ids = lax.broadcasted_iota(jnp.int32, (1, chans, 1, 1), 1)
    depth_ok = depth_valid[:, None, :, :].astype(jnp.float32)
    valid = jnp.where(chan_ids == chans - 1, depth_ok, jnp.float32(1.0))
    resid = ((frames.astype(jnp.float32) - prev_fg.astype(jnp.float32)) * valid).astype(
        jnp.bfloat16
    )
    flat = resid.reshape(count, chans * rows * cols)
    everyone = lax.all_gather(flat, "frame", axis=0, tiled=True)
    block = pair_rows(everyone, flat)
    summed = lax.psum(block, "pix")
    gram = lax.all_gather(summed, "frame", axis=1, tiled=True)
    gram = gram / nval
    mixing = mixing_matrix(gram, sketch)
    mine = lax.dynamic_slice_in_dim(mixing, start_frame, count, 1).astype(jnp.bfloat16)
    back = over_frames(mine, everyone)
    background = back.reshape(count, chans, rows, cols).astype(jnp.bfloat16)
    rounded = lax.optimization_barrier(background).astype(jnp.float32)
    source = (frames.astype(jnp.float32) - rounded) * valid
    lam = tv_weight.reshape(1, chans, 1, 1)
    step = STEP_SIZE / lam
    last_col = lax.broadcasted_iota(jnp.int32, (1, 1, 1, cols), 3) == cols - 1
    row_ids = lax.axis_index("pix") * rows + lax.broadcasted_iota(jnp.int32, (1, 1, rows, 1), 2)
    last_row = row_ids == height - 1

    def divergence(first, second):
        above = from_behind(shortened(first[:, :, -1:, :]), "pix", 1)
        prev_rows = jnp.concatenate([above, first[:, :, :-1, :]], axis=2)
        return first - prev_rows + (second - col_prev(second))

    first = jnp.zeros_like(source)
    second = jnp.zeros_like(source)
    for sweep in range(NSWEEP):
        smooth = source - lam * divergence(first, second)
        below = from_behind(shortened(smooth[:, :, :1, :]), "pix", -1)
        next_rows = jnp.concatenate([smooth[:, :, 1:, :], below], axis=2)
        down = jnp.where(last_row, 0.0, next_rows - smooth)
        across = col_grad(smooth, last_col)
        first, second = dual_update(first, second, down, across, step)
    smooth = source - lam * divergence(first, second)
    return (background, smooth.astype(jnp.bfloat16))


def solution(mesh):
    placed = (
        P("frame", None, "pix", None),
        P("frame", None, "pix", None),
        P("frame", "pix", None),
        P(),
        P(),
    )
    return jax.shard_map(
        local,
        mesh=mesh,
        in_specs=placed,
        out_specs=(P("frame", None, "pix", None), P("frame", None, "pix", None)),
        check_vma=False,
    )
```

profile of v0, /device:TPU:8, one launch (start us, length us, event | category | flops | bytes accessed | tf_op | source)
XLA Modules:
  0.0 442.0 jit_solution(11430136703876754686)
XLA Ops:
  17.5 82.8 %all-gather.2.cloned.1.call-done = bf16[128,32768]{1,0:T(8,128)(2,1)} async-done(((bf16[32,32768]{1,0:T(8,128)(2,1)}), bf16[128,32768]{1,0:T(8,128)(2,1)}) %all-gather.2.cloned.1.call-update) | async-done | bytes 8388624 | tf_op jit(solution)/shard_map/all_gather | solution.py:87
  100.3 6.9 %fusion.61 = f32[128,32]{0,1:T(8,128)S(1)} fusion(bf16[128,32768]{1,0:T(8,128)(2,1)} %all-gather.2.cloned.1.call-done, bf16[32,32768]{1,0:T(8,128)(2,1)} %bitcast.91), kind=kOutput, calls=%fused_computation.132 | convolution fusion | flops 268435456 | bytes 10502144 | tf_op jit(solution)/shard_map/dot_general | solution.py:49
  107.2 110.5 %psum.7 = f32[128,32]{0,1:T(8,128)S(1)} all-reduce(f32[128,32]{0,1:T(8,128)S(1)} %fusion.61), channel_id=1, replica_groups=mesh['frame'=4,'pix'=32] {'pix'}, use_global_device_ids=true, to_apply=%region_0.1 | all-reduce | flops 4096 | bytes 32768 | tf_op jit(solution)/shard_map/psum | solution.py:89
  217.7 12.0 %all_gather.7 = f32[128,128]{0,1:T(8,128)S(1)} all-gather(f32[128,32]{0,1:T(8,128)S(1)} %psum.7), channel_id=1, replica_groups=mesh['frame'=4,'pix'=32] {'frame'}, dimensions={1}, use_global_device_ids=true | all-gather | bytes 81920 | tf_op jit(solution)/shard_map/all_gather | solution.py:90
  230.2 5.8 %cholesky.74 = f32[64,64]{1,0:T(8,128)S(1)} custom-call(f32[64,64]{1,0:T(8,128)S(1)} %add_multiply_fusion), custom_call_target="Cholesky" | custom-call | tf_op jit(solution)/shard_map/jit(cholesky)/cholesky | solution.py:33
  243.0 5.8 %cholesky.85 = f32[64,64]{1,0:T(8,128)S(1)} custom-call(f32[64,64]{1,0:T(8,128)S(1)} %fusion.44), custom_call_target="Cholesky" | custom-call | tf_op jit(solution)/shard_map/jit(cholesky)/cholesky | solution.py:33
  250.2 4.9 %custom-call.14 = f32[1,64,64]{1,2,0:T(8,128)S(1)} custom-call(f32[1,64,64]{2,1,0:T(8,128)S(1)} %fusion.33), custom_call_target="InvertDiagBlocksLowerTriangular" | custom-call | tf_op jit(solution)/shard_map/triangular_solve/custom-call.0 | solution.py:34
  255.8 5.8 %cholesky.96 = f32[64,64]{1,0:T(8,128)S(1)} custom-call(f32[64,64]{1,0:T(8,128)S(1)} %fusion.42), custom_call_target="Cholesky" | custom-call | tf_op jit(solution)/shard_map/jit(cholesky)/cholesky | solution.py:33
  263.0 4.9 %custom-call.15 = f32[1,64,64]{1,2,0:T(8,128)S(1)} custom-call(f32[1,64,64]{2,1,0:T(8,128)S(1)} %fusion.34), custom_call_target="InvertDiagBlocksLowerTriangular" | custom-call | tf_op jit(solution)/shard_map/triangular_solve/custom-call.0 | solution.py:34
  268.9 5.8 %cholesky.107 = f32[64,64]{1,0:T(8,128)S(1)} custom-call(f32[64,64]{1,0:T(8,128)S(1)} %fusion.40), custom_call_target="Cholesky" | custom-call | tf_op jit(solution)/shard_map/jit(cholesky)/cholesky | solution.py:38
  305.6 7.1 %collective-permute-done.2 = bf16[32,4,1,512]{3,0,2,1:T(8,128)(2,1)S(1)} collective-permute-done((bf16[32,4,1,512]{3,0,2,1:T(8,128)(2,1)S(1)}, bf16[32,4,1,512]{3,0,2,1:T(8,128)(2,1)S(1)}, u32[]{:S(2)}, u32[]{:S(2)}) %collective-permute-start.2) | collective-permute-done | bytes 131104 | tf_op jit(solution)/shard_map/ppermute | solution.py:22
  312.8 5.2 %fusion.4 = f32[32,4,16,512]{3,0,2,1:T(8,128)S(1)} fusion(f32[32,4,16,512]{3,0,2,1:T(8,128)S(1)} %get-tuple-element.17, f32[32,4,15,512]{3,0,2,1:T(8,128)S(1)} %slice.153, f32[32,4,1,512]{3,0,2,1:T(8,128)S(1)} %convert_element_type.96, f32[32,4,16,512]{3,0,2,1:T(8,128)S(1)} %get-tuple-element.16, f32[32,4,16,511]{3,0,2,1:T(8,128)S(1)} %bitcast.88, ...), kind=kLoop, calls=%fused_computation.11 | loop fusion | flops 11534336 | bytes 26206228 | tf_op jit(solution)/shard_map/sub | solution.py:112
  325.7 5.9 %subtract_divide_fusion.6 = (f32[32,4,16,512]{3,0,2,1:T(8,128)S(1)}, f32[32,4,16,512]{3,0,2,1:T(8,128)S(1)}) fusion(f32[32,4,16,512]{3,0,2,1:T(8,128)S(1)} %get-tuple-element.16, f32[4]{0:T(128)S(1)} %broadcast_divide_fusion, f32[32,4,16,512]{3,0,2,1:T(8,128)S(1)} %fusion.4, f32[32,4,16,511]{3,0,2,1:T(8,128)} %slice.157, ...), kind=kLoop, calls=%fused_computation.49 | loop fusion | flops 16777216 | bytes 29352480 | tf_op jit(solution)/shard_map/div | solution.py:63
  335.1 6.7 %collective-permute-done.4 = bf16[32,4,1,512]{3,0,2,1:T(8,128)(2,1)S(1)} collective-permute-done((bf16[32,4,1,512]{3,0,2,1:T(8,128)(2,1)S(1)}, bf16[32,4,1,512]{3,0,2,1:T(8,128)(2,1)S(1)}, u32[]{:S(2)}, u32[]{:S(2)}) %collective-permute-start.4) | collective-permute-done | bytes 131104 | tf_op jit(solution)/shard_map/ppermute | solution.py:22
  341.8 5.2 %fusion.8 = f32[32,4,16,512]{3,0,2,1:T(8,128)S(1)} fusion(f32[32,4,16,512]{3,0,2,1:T(8,128)S(1)} %get-tuple-element.15, f32[32,4,15,512]{3,0,2,1:T(8,128)S(1)} %slice.159, f32[32,4,1,512]{3,0,2,1:T(8,128)S(1)} %convert_element_type.98, f32[32,4,16,512]{3,0,2,1:T(8,128)S(1)} %get-tuple-element.14, f32[32,4,16,511]{3,0,2,1:T(8,128)S(1)} %bitcast.86, ...), kind=kLoop, calls=%fused_computation.17 | loop fusion | flops 11534336 | bytes 26206228 | tf_op jit(solution)/shard_map/sub | solution.py:112
  354.7 5.9 %subtract_divide_fusion.4 = (f32[32,4,16,512]{3,0,2,1:T(8,128)S(1)}, f32[32,4,16,512]{3,0,2,1:T(8,128)S(1)}) fusion(f32[32,4,16,512]{3,0,2,1:T(8,128)S(1)} %get-tuple-element.14, f32[4]{0:T(128)S(1)} %broadcast_divide_fusion, f32[32,4,16,512]{3,0,2,1:T(8,128)S(1)} %fusion.8, f32[32,4,16,511]{3,0,2,1:T(8,128)} %slice.163, ...), kind=kLoop, calls=%fused_computation.45 | loop fusion | flops 16777216 | bytes 29352480 | tf_op jit(solution)/shard_map/div | solution.py:63
  363.8 7.1 %collective-permute-done.6 = bf16[32,4,1,512]{3,0,2,1:T(8,128)(2,1)S(1)} collective-permute-done((bf16[32,4,1,512]{3,0,2,1:T(8,128)(2,1)S(1)}, bf16[32,4,1,512]{3,0,2,1:T(8,128)(2,1)S(1)}, u32[]{:S(2)}, u32[]{:S(2)}) %collective-permute-start.6) | collective-permute-done | bytes 131104 | tf_op jit(solution)/shard_map/ppermute | solution.py:22
  370.9 5.2 %fusion.12 = f32[32,4,16,512]{3,0,2,1:T(8,128)S(1)} fusion(f32[32,4,16,512]{3,0,2,1:T(8,128)S(1)} %get-tuple-element.13, f32[32,4,15,512]{3,0,2,1:T(8,128)S(1)} %slice.165, f32[32,4,1,512]{3,0,2,1:T(8,128)S(1)} %convert_element_type.100, f32[32,4,16,512]{3,0,2,1:T(8,128)S(1)} %get-tuple-element.12, f32[32,4,16,511]{3,0,2,1:T(8,128)S(1)} %bitcast.87, ...), kind=kLoop, calls=%fused_computation.23 | loop fusion | flops 11534336 | bytes 26206228 | tf_op jit(solution)/shard_map/sub | solution.py:112
  383.9 5.9 %subtract_divide_fusion.2 = (f32[32,4,16,512]{3,0,2,1:T(8,128)S(1)}, f32[32,4,16,512]{3,0,2,1:T(8,128)S(1)}) fusion(f32[32,4,16,512]{3,0,2,1:T(8,128)S(1)} %get-tuple-element.12, f32[4]{0:T(128)S(1)} %broadcast_divide_fusion, f32[32,4,16,512]{3,0,2,1:T(8,128)S(1)} %fusion.12, f32[32,4,16,511]{3,0,2,1:T(8,128)} %slice.169, ...), kind=kLoop, calls=%fused_computation.41 | loop fusion | flops 16777216 | bytes 29352480 | tf_op jit(solution)/shard_map/div | solution.py:63
  393.0 7.1 %collective-permute-done.8 = bf16[32,4,1,512]{3,0,2,1:T(8,128)(2,1)S(1)} collective-permute-done((bf16[32,4,1,512]{3,0,2,1:T(8,128)(2,1)S(1)}, bf16[32,4,1,512]{3,0,2,1:T(8,128)(2,1)S(1)}, u32[]{:S(2)}, u32[]{:S(2)}) %collective-permute-start.8) | collective-permute-done | bytes 131104 | tf_op jit(solution)/shard_map/ppermute | solution.py:22
  400.1 5.2 %fusion.16 = f32[32,4,16,512]{3,0,2,1:T(8,128)S(1)} fusion(f32[32,4,16,512]{3,0,2,1:T(8,128)S(1)} %get-tuple-element.11, f32[32,4,15,512]{3,0,2,1:T(8,128)S(1)} %slice.171, f32[32,4,1,512]{3,0,2,1:T(8,128)S(1)} %convert_element_type.102, f32[32,4,16,512]{3,0,2,1:T(8,128)S(1)} %get-tuple-element.10, f32[32,4,16,511]{3,0,2,1:T(8,128)S(1)} %bitcast.85, ...), kind=kLoop, calls=%fused_computation.29 | loop fusion | flops 11534336 | bytes 26206228 | tf_op jit(solution)/shard_map/sub | solution.py:112
  413.0 5.9 %subtract_divide_fusion = (f32[32,4,16,512]{3,0,2,1:T(8,128)S(1)}, f32[32,4,16,512]{3,0,2,1:T(8,128)S(1)}) fusion(f32[32,4,16,512]{3,0,2,1:T(8,128)S(1)} %get-tuple-element.10, f32[4]{0:T(128)S(1)} %broadcast_divide_fusion, f32[32,4,16,512]{3,0,2,1:T(8,128)S(1)} %fusion.16, f32[32,4,16,511]{3,0,2,1:T(8,128)} %slice.175, ...), kind=kLoop, calls=%fused_computation.37 | loop fusion | flops 16777216 | bytes 29352480 | tf_op jit(solution)/shard_map/div | solution.py:63
  422.3 5.0 %collective-permute-done.10 = bf16[32,4,1,512]{3,0,2,1:T(8,128)(2,1)S(1)} collective-permute-done((bf16[32,4,1,512]{3,0,2,1:T(8,128)(2,1)S(1)}, bf16[32,4,1,512]{3,0,2,1:T(8,128)(2,1)S(1)}, u32[]{:S(2)}, u32[]{:S(2)}) %collective-permute-start.10) | collective-permute-done | bytes 131104 | tf_op jit(solution)/shard_map/ppermute | solution.py:22
  427.3 5.1 %fusion.21 = bf16[32,4,16,512]{3,0,2,1:T(8,128)(2,1)S(1)} fusion(f32[32,4,16,512]{3,0,2,1:T(8,128)S(1)} %get-tuple-element.9, f32[32,4,15,512]{3,0,2,1:T(8,128)S(1)} %slice.177, f32[32,4,1,512]{3,0,2,1:T(8,128)S(1)} %convert_element_type.104, f32[32,4,16,512]{3,0,2,1:T(8,128)S(1)} %get-tuple-element.8, f32[32,4,16,511]{3,0,2,1:T(8,128)S(1)} %bitcast.89, ...), kind=kLoop, calls=%fused_computation.36 | loop fusion | flops 12582912 | bytes 24109076 | tf_op jit(solution)/shard_map/convert_element_type | solution.py:119
  (126 shorter events, 99.2 us)
Async XLA Ops:
  7.2 222.6 %copy-start = (f32[128,64]{0,1:T(8,128)S(1)}, f32[128,64]{0,1:T(8,128)}, u32[]{:S(2)}) copy-start(f32[128,64]{0,1:T(8,128)} %param.11) | copy-start | bytes 98308
  7.2 2.2 copy-start.2
  7.2 93.1 %all-gather.2.cloned.1.call-start = ((), (), s32[]{:S(2)}) async-start(), calls=%async_computation | async-start | bytes 10485760 | tf_op jit(solution)/shard_map/all_gather | solution.py:87
  7.2 2.5 copy-start.7
  13.3 4.2 copy-start.8
  15.5 271.5 %collective-permute-start = (bf16[32,4,1,512]{3,0,2,1:T(8,128)(2,1)}, bf16[32,4,1,512]{3,0,2,1:T(8,128)(2,1)S(1)}, u32[]{:S(2)}, u32[]{:S(2)}) collective-permute-start(bf16[32,4,1,512]{3,0,2,1:T(8,128)(2,1)} %convert_element_type.94), channel_id=1, source_target_pairs={{0,1},{1,2},{2,3},{3,4},{4,5},{5,6},{6,7},{7,8},{8,9},{9,10},{10,1... | collective-permute-start | bytes 393224 | tf_op jit(solution)/shard_map/ppermute | solution.py:22
  287.0 3.5 copy-start.3
  290.5 1.9 copy-start.5
  292.5 5.3 %collective-permute-start.1 = (bf16[32,4,1,512]{3,0,2,1:T(8,128)(2,1)S(1)}, bf16[32,4,1,512]{3,0,2,1:T(8,128)(2,1)S(1)}, u32[]{:S(2)}, u32[]{:S(2)}) collective-permute-start(bf16[32,4,1,512]{3,0,2,1:T(8,128)(2,1)S(1)} %slice.198), channel_id=1, source_target_pairs={{1,0},{2,1},{3,2},{4,3},{5,4},{6,5},{7,6},{8,7},{9,8},{10,9},{11,1... | collective-permute-start | bytes 393224 | tf_op jit(solution)/shard_map/ppermute | solution.py:22
  294.4 2.2 copy-start.6
  296.6 2.1 slice-start
  302.4 10.4 %copy-start.4 = (bf16[4,8,64,512]{3,2,1,0:T(8,128)(2,1)S(1)}, bf16[4,8,64,512]{3,2,1,0:T(8,128)(2,1)}, u32[]{:S(2)}) copy-start(bf16[4,8,64,512]{3,2,1,0:T(8,128)(2,1)} %copy-done.3) | copy-start | bytes 6291460
  302.4 10.4 %collective-permute-start.2 = (bf16[32,4,1,512]{3,0,2,1:T(8,128)(2,1)S(1)}, bf16[32,4,1,512]{3,0,2,1:T(8,128)(2,1)S(1)}, u32[]{:S(2)}, u32[]{:S(2)}) collective-permute-start(bf16[32,4,1,512]{3,0,2,1:T(8,128)(2,1)S(1)} %slice.197), channel_id=1, source_target_pairs={{0,1},{1,2},{2,3},{3,4},{4,5},{5,6},{6,7},{7,8},{8,9},{9,10},{10,1... | collective-permute-start | bytes 393224 | tf_op jit(solution)/shard_map/ppermute | solution.py:22
  318.0 7.6 %collective-permute-start.3 = (bf16[32,4,1,512]{3,0,2,1:T(8,128)(2,1)S(1)}, bf16[32,4,1,512]{3,0,2,1:T(8,128)(2,1)S(1)}, u32[]{:S(2)}, u32[]{:S(2)}) collective-permute-start(bf16[32,4,1,512]{3,0,2,1:T(8,128)(2,1)S(1)} %slice.196), channel_id=1, source_target_pairs={{1,0},{2,1},{3,2},{4,3},{5,4},{6,5},{7,6},{8,7},{9,8},{10,9},{11,1... | collective-permute-start | bytes 393224 | tf_op jit(solution)/shard_map/ppermute | solution.py:22
  331.6 10.2 %collective-permute-start.4 = (bf16[32,4,1,512]{3,0,2,1:T(8,128)(2,1)S(1)}, bf16[32,4,1,512]{3,0,2,1:T(8,128)(2,1)S(1)}, u32[]{:S(2)}, u32[]{:S(2)}) collective-permute-start(bf16[32,4,1,512]{3,0,2,1:T(8,128)(2,1)S(1)} %slice.195), channel_id=1, source_target_pairs={{0,1},{1,2},{2,3},{3,4},{4,5},{5,6},{6,7},{7,8},{8,9},{9,10},{10,1... | collective-permute-start | bytes 393224 | tf_op jit(solution)/shard_map/ppermute | solution.py:22
  347.1 7.6 %collective-permute-start.5 = (bf16[32,4,1,512]{3,0,2,1:T(8,128)(2,1)S(1)}, bf16[32,4,1,512]{3,0,2,1:T(8,128)(2,1)S(1)}, u32[]{:S(2)}, u32[]{:S(2)}) collective-permute-start(bf16[32,4,1,512]{3,0,2,1:T(8,128)(2,1)S(1)} %slice.194), channel_id=1, source_target_pairs={{1,0},{2,1},{3,2},{4,3},{5,4},{6,5},{7,6},{8,7},{9,8},{10,9},{11,1... | collective-permute-start | bytes 393224 | tf_op jit(solution)/shard_map/ppermute | solution.py:22
  360.6 10.2 %collective-permute-start.6 = (bf16[32,4,1,512]{3,0,2,1:T(8,128)(2,1)S(1)}, bf16[32,4,1,512]{3,0,2,1:T(8,128)(2,1)S(1)}, u32[]{:S(2)}, u32[]{:S(2)}) collective-permute-start(bf16[32,4,1,512]{3,0,2,1:T(8,128)(2,1)S(1)} %slice.193), channel_id=1, source_target_pairs={{0,1},{1,2},{2,3},{3,4},{4,5},{5,6},{6,7},{7,8},{8,9},{9,10},{10,1... | collective-permute-start | bytes 393224 | tf_op jit(solution)/shard_map/ppermute | solution.py:22
  376.1 7.8 %collective-permute-start.7 = (bf16[32,4,1,512]{3,0,2,1:T(8,128)(2,1)S(1)}, bf16[32,4,1,512]{3,0,2,1:T(8,128)(2,1)S(1)}, u32[]{:S(2)}, u32[]{:S(2)}) collective-permute-start(bf16[32,4,1,512]{3,0,2,1:T(8,128)(2,1)S(1)} %slice.192), channel_id=1, source_target_pairs={{1,0},{2,1},{3,2},{4,3},{5,4},{6,5},{7,6},{8,7},{9,8},{10,9},{11,1... | collective-permute-start | bytes 393224 | tf_op jit(solution)/shard_map/ppermute | solution.py:22
  389.8 10.2 %collective-permute-start.8 = (bf16[32,4,1,512]{3,0,2,1:T(8,128)(2,1)S(1)}, bf16[32,4,1,512]{3,0,2,1:T(8,128)(2,1)S(1)}, u32[]{:S(2)}, u32[]{:S(2)}) collective-permute-start(bf16[32,4,1,512]{3,0,2,1:T(8,128)(2,1)S(1)} %slice.191), channel_id=1, source_target_pairs={{0,1},{1,2},{2,3},{3,4},{4,5},{5,6},{6,7},{7,8},{8,9},{9,10},{10,1... | collective-permute-start | bytes 393224 | tf_op jit(solution)/shard_map/ppermute | solution.py:22
  405.4 7.6 %collective-permute-start.9 = (bf16[32,4,1,512]{3,0,2,1:T(8,128)(2,1)S(1)}, bf16[32,4,1,512]{3,0,2,1:T(8,128)(2,1)S(1)}, u32[]{:S(2)}, u32[]{:S(2)}) collective-permute-start(bf16[32,4,1,512]{3,0,2,1:T(8,128)(2,1)S(1)} %slice.190), channel_id=1, source_target_pairs={{1,0},{2,1},{3,2},{4,3},{5,4},{6,5},{7,6},{8,7},{9,8},{10,9},{11,1... | collective-permute-start | bytes 393224 | tf_op jit(solution)/shard_map/ppermute | solution.py:22
  418.9 8.4 %collective-permute-start.10 = (bf16[32,4,1,512]{3,0,2,1:T(8,128)(2,1)S(1)}, bf16[32,4,1,512]{3,0,2,1:T(8,128)(2,1)S(1)}, u32[]{:S(2)}, u32[]{:S(2)}) collective-permute-start(bf16[32,4,1,512]{3,0,2,1:T(8,128)(2,1)S(1)} %slice.189), channel_id=1, source_target_pairs={{0,1},{1,2},{2,3},{3,4},{4,5},{5,6},{6,7},{7,8},{8,9},{9,10},{10,1... | collective-permute-start | bytes 393224 | tf_op jit(solution)/shard_map/ppermute | solution.py:22
  427.3 7.6 %copy-start.1 = (f32[128,64]{0,1:T(8,128)S(1)}, f32[128,64]{0,1:T(8,128)}, u32[]{:S(2)}) copy-start(f32[128,64]{0,1:T(8,128)} %param.11) | copy-start | bytes 98308
Sparse Core Ops, SparseCore 0:
  15.0 85.3 all-gather.1
where the time goes:
time: 448 us; the launch traced here: 442 us
  blocking collectives  122 us (27%)
  waiting for transfers between devices  116 us (26%)
  other arithmetic  110 us (25%)
  local copies, waits for them, and re-layouts  39.3 us (9%)
  starting transfers between devices  24.5 us (5%)
  between operations  15 us (3%)
  matrix products  14.7 us (3%)
    psum x1, blocking collectives, local(): summed = lax.psum(block, 'pix')  110 us
    all_gather x1, waiting for transfers between devices, local(): everyone = lax.all_gather(flat, 'frame', axis=0, tiled=True)  82.8 us
    ppermute x11, waiting for transfers between devices, from_behind(): lax.ppermute(value, axis, [(source, source + steps) for source in range(l...  33 us
    div x5, other arithmetic, dual_update(): return ((first - step * down) / scale, (second - step * across) / scale)  27.1 us
    another operation x12, other arithmetic, mixing_matrix(): factor = jnp.linalg.cholesky(exact_dot(basis.T, image))  26.1 us
    ppermute x11, starting transfers between devices, from_behind(): lax.ppermute(value, axis, [(source, source + steps) for source in range(l...  24.5 us
    sub x5, other arithmetic, local(): smooth = source - lam * divergence(first, second)  24.3 us
    another operation x6, other arithmetic, mixing_matrix(): lax.linalg.triangular_solve(factor, image, left_side=False, lower=True, t...  16.6 us
  transfers between devices with their start and end apart: 12, of which 6 were waited for; matrix products, arithmetic and copies ran while one was open for 21% of the time, Pallas kernels for 0%

commit v1 on v0

--- a/solution.py
+++ b/solution.py
@@ -86,7 +86,7 @@
     flat = resid.reshape(count, chans * rows * cols)
     everyone = lax.all_gather(flat, "frame", axis=0, tiled=True)
     block = pair_rows(everyone, flat)
-    summed = lax.psum(block, "pix")
+    summed = jnp.sum(lax.all_gather(block, "pix"), axis=0)
     gram = lax.all_gather(summed, "frame", axis=1, tiled=True)
     gram = gram / nval
     mixing = mixing_matrix(gram, sketch)

time: 448 us -> 356 us (0.79)
  blocking collectives: 122 us -> 36.8 us
  waiting for transfers between devices: 116 us -> 108 us
    psum x1 -> x0, blocking collectives: 110 us -> none  [local(): summed = lax.psum(block, 'pix')]
    all_gather x0 -> x1, blocking collectives: none -> 24.8 us  [local(): summed = jnp.sum(lax.all_gather(block, 'pix'), axis=0)]
    ppermute x11, waiting for transfers between devices: 33 us -> 25.7 us  [from_behind(): lax.ppermute(value, axis, [(source, source + steps) for source in range(l...]
    unnamed x21 -> x22, local copies, waits for them, and re-layouts: 9.14 us -> 9.24 us
  transfers between devices with their start and end apart: 12 -> 12, of which waited for: 6 -> 6; matrix products, arithmetic and copies ran while one was open for 21% -> 26% of each run, Pallas kernels for 0% -> 0%
where the time goes in v1:
time: 356 us; the launch traced here: 349 us
  other arithmetic  110 us (31%)
  waiting for transfers between devices  108 us (30%)
  local copies, waits for them, and re-layouts  39.4 us (11%)
  blocking collectives  36.8 us (10%)
  starting transfers between devices  24.5 us (7%)
  between operations  15 us (4%)
  matrix products  14.7 us (4%)
    all_gather x1, waiting for transfers between devices, local(): everyone = lax.all_gather(flat, 'frame', axis=0, tiled=True)  82.8 us
    div x5, other arithmetic, dual_update(): return ((first - step * down) / scale, (second - step * across) / scale)  27.1 us
    another operation x12, other arithmetic, mixing_matrix(): factor = jnp.linalg.cholesky(exact_dot(basis.T, image))  26.1 us
    ppermute x11, waiting for transfers between devices, from_behind(): lax.ppermute(value, axis, [(source, source + steps) for source in range(l...  25.7 us
    all_gather x1, blocking collectives, local(): summed = jnp.sum(lax.all_gather(block, 'pix'), axis=0)  24.8 us
    ppermute x11, starting transfers between devices, from_behind(): lax.ppermute(value, axis, [(source, source + steps) for source in range(l...  24.5 us
    sub x5, other arithmetic, local(): smooth = source - lam * divergence(first, second)  24.3 us
    another operation x6, other arithmetic, mixing_matrix(): lax.linalg.triangular_solve(factor, image, left_side=False, lower=True, t...  16.6 us
  transfers between devices with their start and end apart: 12, of which 6 were waited for; matrix products, arithmetic and copies ran while one was open for 26% of the time, Pallas kernels for 0%

profile of v1, /device:TPU:8, one launch (start us, length us, event | category | flops | bytes accessed | tf_op | source)
XLA Modules:
  0.0 349.2 jit_solution(13859566698846477198)
XLA Ops:
  17.5 82.8 %all-gather.3.cloned.1.call-done = bf16[128,32768]{1,0:T(8,128)(2,1)} async-done(((bf16[32,32768]{1,0:T(8,128)(2,1)}), bf16[128,32768]{1,0:T(8,128)(2,1)}) %all-gather.3.cloned.1.call-update) | async-done | bytes 8388624 | tf_op jit(solution)/shard_map/all_gather | solution.py:87
  100.3 6.9 %fusion.61 = f32[128,32]{0,1:T(8,128)S(1)} fusion(bf16[128,32768]{1,0:T(8,128)(2,1)} %all-gather.3.cloned.1.call-done, bf16[32,32768]{1,0:T(8,128)(2,1)} %bitcast.96), kind=kOutput, calls=%fused_computation.133 | convolution fusion | flops 268435456 | bytes 10502144 | tf_op jit(solution)/shard_map/dot_general | solution.py:49
  107.2 24.8 %all-gather = f32[4096,32]{0,1:T(8,128)S(1)} all-gather(f32[128,32]{0,1:T(8,128)S(1)} %fusion.61), channel_id=2, replica_groups=mesh['frame'=4,'pix'=32] {'pix'}, dimensions={0}, use_global_device_ids=true | all-gather | bytes 540672 | tf_op jit(solution)/shard_map/all_gather | solution.py:89
  132.1 12.0 %all_gather.15 = f32[128,128]{0,1:T(8,128)S(1)} all-gather(f32[128,32]{0,1:T(8,128)S(1)} %bitcast_reduce_fusion), channel_id=1, replica_groups=mesh['frame'=4,'pix'=32] {'frame'}, dimensions={1}, use_global_device_ids=true | all-gather | bytes 81920 | tf_op jit(solution)/shard_map/all_gather | solution.py:90
  144.7 5.8 %cholesky.74 = f32[64,64]{1,0:T(8,128)S(1)} custom-call(f32[64,64]{1,0:T(8,128)S(1)} %add_multiply_fusion), custom_call_target="Cholesky" | custom-call | tf_op jit(solution)/shard_map/jit(cholesky)/cholesky | solution.py:33
  151.9 4.9 %custom-call.13 = f32[1,64,64]{1,2,0:T(8,128)S(1)} custom-call(f32[1,64,64]{2,1,0:T(8,128)S(1)} %fusion.32), custom_call_target="InvertDiagBlocksLowerTriangular" | custom-call | tf_op jit(solution)/shard_map/triangular_solve/custom-call.0 | solution.py:34
  157.5 5.8 %cholesky.85 = f32[64,64]{1,0:T(8,128)S(1)} custom-call(f32[64,64]{1,0:T(8,128)S(1)} %fusion.44), custom_call_target="Cholesky" | custom-call | tf_op jit(solution)/shard_map/jit(cholesky)/cholesky | solution.py:33
  164.7 4.9 %custom-call.14 = f32[1,64,64]{1,2,0:T(8,128)S(1)} custom-call(f32[1,64,64]{2,1,0:T(8,128)S(1)} %fusion.33), custom_call_target="InvertDiagBlocksLowerTriangular" | custom-call | tf_op jit(solution)/shard_map/triangular_solve/custom-call.0 | solution.py:34
  170.3 5.8 %cholesky.96 = f32[64,64]{1,0:T(8,128)S(1)} custom-call(f32[64,64]{1,0:T(8,128)S(1)} %fusion.42), custom_call_target="Cholesky" | custom-call | tf_op jit(solution)/shard_map/jit(cholesky)/cholesky | solution.py:33
  177.5 4.9 %custom-call.15 = f32[1,64,64]{1,2,0:T(8,128)S(1)} custom-call(f32[1,64,64]{2,1,0:T(8,128)S(1)} %fusion.34), custom_call_target="InvertDiagBlocksLowerTriangular" | custom-call | tf_op jit(solution)/shard_map/triangular_solve/custom-call.0 | solution.py:34
  183.4 5.8 %cholesky.107 = f32[64,64]{1,0:T(8,128)S(1)} custom-call(f32[64,64]{1,0:T(8,128)S(1)} %fusion.40), custom_call_target="Cholesky" | custom-call | tf_op jit(solution)/shard_map/jit(cholesky)/cholesky | solution.py:38
  220.1 5.3 %collective-permute-done.2 = bf16[32,4,1,512]{3,0,2,1:T(8,128)(2,1)S(1)} collective-permute-done((bf16[32,4,1,512]{3,0,2,1:T(8,128)(2,1)S(1)}, bf16[32,4,1,512]{3,0,2,1:T(8,128)(2,1)S(1)}, u32[]{:S(2)}, u32[]{:S(2)}) %collective-permute-start.2) | collective-permute-done | bytes 131104 | tf_op jit(solution)/shard_map/ppermute | solution.py:22
  225.4 5.2 %fusion.4 = f32[32,4,16,512]{3,0,2,1:T(8,128)S(1)} fusion(f32[32,4,16,512]{3,0,2,1:T(8,128)S(1)} %get-tuple-element.17, f32[32,4,15,512]{3,0,2,1:T(8,128)S(1)} %slice.153, f32[32,4,1,512]{3,0,2,1:T(8,128)S(1)} %convert_element_type.96, f32[32,4,16,512]{3,0,2,1:T(8,128)S(1)} %get-tuple-element.16, f32[32,4,16,511]{3,0,2,1:T(8,128)S(1)} %bitcast.93, ...), kind=kLoop, calls=%fused_computation.11 | loop fusion | flops 11534336 | bytes 26206228 | tf_op jit(solution)/shard_map/sub | solution.py:112
  238.3 5.9 %subtract_divide_fusion.6 = (f32[32,4,16,512]{3,0,2,1:T(8,128)S(1)}, f32[32,4,16,512]{3,0,2,1:T(8,128)S(1)}) fusion(f32[32,4,16,512]{3,0,2,1:T(8,128)S(1)} %get-tuple-element.16, f32[4]{0:T(128)S(1)} %broadcast_divide_fusion, f32[32,4,16,512]{3,0,2,1:T(8,128)S(1)} %fusion.4, f32[32,4,16,511]{3,0,2,1:T(8,128)} %slice.157, ...), kind=kLoop, calls=%fused_computation.49 | loop fusion | flops 16777216 | bytes 29352480 | tf_op jit(solution)/shard_map/div | solution.py:63
  252.6 5.2 %fusion.8 = f32[32,4,16,512]{3,0,2,1:T(8,128)S(1)} fusion(f32[32,4,16,512]{3,0,2,1:T(8,128)S(1)} %get-tuple-element.15, f32[32,4,15,512]{3,0,2,1:T(8,128)S(1)} %slice.159, f32[32,4,1,512]{3,0,2,1:T(8,128)S(1)} %convert_element_type.98, f32[32,4,16,512]{3,0,2,1:T(8,128)S(1)} %get-tuple-element.14, f32[32,4,16,511]{3,0,2,1:T(8,128)S(1)} %bitcast.91, ...), kind=kLoop, calls=%fused_computation.17 | loop fusion | flops 11534336 | bytes 26206228 | tf_op jit(solution)/shard_map/sub | solution.py:112
  265.5 5.9 %subtract_divide_fusion.4 = (f32[32,4,16,512]{3,0,2,1:T(8,128)S(1)}, f32[32,4,16,512]{3,0,2,1:T(8,128)S(1)}) fusion(f32[32,4,16,512]{3,0,2,1:T(8,128)S(1)} %get-tuple-element.14, f32[4]{0:T(128)S(1)} %broadcast_divide_fusion, f32[32,4,16,512]{3,0,2,1:T(8,128)S(1)} %fusion.8, f32[32,4,16,511]{3,0,2,1:T(8,128)} %slice.163, ...), kind=kLoop, calls=%fused_computation.45 | loop fusion | flops 16777216 | bytes 29352480 | tf_op jit(solution)/shard_map/div | solution.py:63
  274.6 5.3 %collective-permute-done.6 = bf16[32,4,1,512]{3,0,2,1:T(8,128)(2,1)S(1)} collective-permute-done((bf16[32,4,1,512]{3,0,2,1:T(8,128)(2,1)S(1)}, bf16[32,4,1,512]{3,0,2,1:T(8,128)(2,1)S(1)}, u32[]{:S(2)}, u32[]{:S(2)}) %collective-permute-start.6) | collective-permute-done | bytes 131104 | tf_op jit(solution)/shard_map/ppermute | solution.py:22
  279.9 5.2 %fusion.12 = f32[32,4,16,512]{3,0,2,1:T(8,128)S(1)} fusion(f32[32,4,16,512]{3,0,2,1:T(8,128)S(1)} %get-tuple-element.13, f32[32,4,15,512]{3,0,2,1:T(8,128)S(1)} %slice.165, f32[32,4,1,512]{3,0,2,1:T(8,128)S(1)} %convert_element_type.100, f32[32,4,16,512]{3,0,2,1:T(8,128)S(1)} %get-tuple-element.12, f32[32,4,16,511]{3,0,2,1:T(8,128)S(1)} %bitcast.92, ...), kind=kLoop, calls=%fused_computation.23 | loop fusion | flops 11534336 | bytes 26206228 | tf_op jit(solution)/shard_map/sub | solution.py:112
  292.9 5.9 %subtract_divide_fusion.2 = (f32[32,4,16,512]{3,0,2,1:T(8,128)S(1)}, f32[32,4,16,512]{3,0,2,1:T(8,128)S(1)}) fusion(f32[32,4,16,512]{3,0,2,1:T(8,128)S(1)} %get-tuple-element.12, f32[4]{0:T(128)S(1)} %broadcast_divide_fusion, f32[32,4,16,512]{3,0,2,1:T(8,128)S(1)} %fusion.12, f32[32,4,16,511]{3,0,2,1:T(8,128)} %slice.169, ...), kind=kLoop, calls=%fused_computation.41 | loop fusion | flops 16777216 | bytes 29352480 | tf_op jit(solution)/shard_map/div | solution.py:63
  302.0 5.3 %collective-permute-done.8 = bf16[32,4,1,512]{3,0,2,1:T(8,128)(2,1)S(1)} collective-permute-done((bf16[32,4,1,512]{3,0,2,1:T(8,128)(2,1)S(1)}, bf16[32,4,1,512]{3,0,2,1:T(8,128)(2,1)S(1)}, u32[]{:S(2)}, u32[]{:S(2)}) %collective-permute-start.8) | collective-permute-done | bytes 131104 | tf_op jit(solution)/shard_map/ppermute | solution.py:22
  307.2 5.2 %fusion.16 = f32[32,4,16,512]{3,0,2,1:T(8,128)S(1)} fusion(f32[32,4,16,512]{3,0,2,1:T(8,128)S(1)} %get-tuple-element.11, f32[32,4,15,512]{3,0,2,1:T(8,128)S(1)} %slice.171, f32[32,4,1,512]{3,0,2,1:T(8,128)S(1)} %convert_element_type.102, f32[32,4,16,512]{3,0,2,1:T(8,128)S(1)} %get-tuple-element.10, f32[32,4,16,511]{3,0,2,1:T(8,128)S(1)} %bitcast.90, ...), kind=kLoop, calls=%fused_computation.29 | loop fusion | flops 11534336 | bytes 26206228 | tf_op jit(solution)/shard_map/sub | solution.py:112
  320.1 5.9 %subtract_divide_fusion = (f32[32,4,16,512]{3,0,2,1:T(8,128)S(1)}, f32[32,4,16,512]{3,0,2,1:T(8,128)S(1)}) fusion(f32[32,4,16,512]{3,0,2,1:T(8,128)S(1)} %get-tuple-element.10, f32[4]{0:T(128)S(1)} %broadcast_divide_fusion, f32[32,4,16,512]{3,0,2,1:T(8,128)S(1)} %fusion.16, f32[32,4,16,511]{3,0,2,1:T(8,128)} %slice.175, ...), kind=kLoop, calls=%fused_computation.37 | loop fusion | flops 16777216 | bytes 29352480 | tf_op jit(solution)/shard_map/div | solution.py:63
  329.4 5.0 %collective-permute-done.10 = bf16[32,4,1,512]{3,0,2,1:T(8,128)(2,1)S(1)} collective-permute-done((bf16[32,4,1,512]{3,0,2,1:T(8,128)(2,1)S(1)}, bf16[32,4,1,512]{3,0,2,1:T(8,128)(2,1)S(1)}, u32[]{:S(2)}, u32[]{:S(2)}) %collective-permute-start.10) | collective-permute-done | bytes 131104 | tf_op jit(solution)/shard_map/ppermute | solution.py:22
  334.5 5.1 %fusion.21 = bf16[32,4,16,512]{3,0,2,1:T(8,128)(2,1)S(1)} fusion(f32[32,4,16,512]{3,0,2,1:T(8,128)S(1)} %get-tuple-element.9, f32[32,4,15,512]{3,0,2,1:T(8,128)S(1)} %slice.177, f32[32,4,1,512]{3,0,2,1:T(8,128)S(1)} %convert_element_type.104, f32[32,4,16,512]{3,0,2,1:T(8,128)S(1)} %get-tuple-element.8, f32[32,4,16,511]{3,0,2,1:T(8,128)S(1)} %bitcast.94, ...), kind=kLoop, calls=%fused_computation.36 | loop fusion | flops 12582912 | bytes 24109076 | tf_op jit(solution)/shard_map/convert_element_type | solution.py:119
  (128 shorter events, 99.3 us)
Async XLA Ops:
  7.2 137.0 %copy-start = (f32[128,64]{0,1:T(8,128)S(1)}, f32[128,64]{0,1:T(8,128)}, u32[]{:S(2)}) copy-start(f32[128,64]{0,1:T(8,128)} %param.11) | copy-start | bytes 98308
  7.2 2.2 copy-start.2
  7.2 93.1 %all-gather.3.cloned.1.call-start = ((), (), s32[]{:S(2)}) async-start(), calls=%async_computation | async-start | bytes 10485760 | tf_op jit(solution)/shard_map/all_gather | solution.py:87
  7.2 2.5 copy-start.7
  13.3 4.2 %copy-start.8 = (f32[4]{0:T(128)S(1)}, f32[4]{0:T(128)}, u32[]{:S(2)}) copy-start(f32[4]{0:T(128)} %param.12) | copy-start | bytes 52
  15.5 186.0 %collective-permute-start = (bf16[32,4,1,512]{3,0,2,1:T(8,128)(2,1)}, bf16[32,4,1,512]{3,0,2,1:T(8,128)(2,1)S(1)}, u32[]{:S(2)}, u32[]{:S(2)}) collective-permute-start(bf16[32,4,1,512]{3,0,2,1:T(8,128)(2,1)} %convert_element_type.94), channel_id=1, source_target_pairs={{0,1},{1,2},{2,3},{3,4},{4,5},{5,6},{6,7},{7,8},{8,9},{9,10},{10,1... | collective-permute-start | bytes 393224 | tf_op jit(solution)/shard_map/ppermute | solution.py:22
  201.5 3.5 copy-start.3
  205.0 1.9 copy-start.5
  207.0 5.3 %collective-permute-start.1 = (bf16[32,4,1,512]{3,0,2,1:T(8,128)(2,1)S(1)}, bf16[32,4,1,512]{3,0,2,1:T(8,128)(2,1)S(1)}, u32[]{:S(2)}, u32[]{:S(2)}) collective-permute-start(bf16[32,4,1,512]{3,0,2,1:T(8,128)(2,1)S(1)} %slice.198), channel_id=1, source_target_pairs={{1,0},{2,1},{3,2},{4,3},{5,4},{6,5},{7,6},{8,7},{9,8},{10,9},{11,1... | collective-permute-start | bytes 393224 | tf_op jit(solution)/shard_map/ppermute | solution.py:22
  208.9 2.2 copy-start.6
  211.1 2.1 slice-start
  216.8 8.6 %copy-start.4 = (bf16[4,8,64,512]{3,2,1,0:T(8,128)(2,1)S(1)}, bf16[4,8,64,512]{3,2,1,0:T(8,128)(2,1)}, u32[]{:S(2)}) copy-start(bf16[4,8,64,512]{3,2,1,0:T(8,128)(2,1)} %copy-done.3) | copy-start | bytes 6291460
  216.9 8.5 %collective-permute-start.2 = (bf16[32,4,1,512]{3,0,2,1:T(8,128)(2,1)S(1)}, bf16[32,4,1,512]{3,0,2,1:T(8,128)(2,1)S(1)}, u32[]{:S(2)}, u32[]{:S(2)}) collective-permute-start(bf16[32,4,1,512]{3,0,2,1:T(8,128)(2,1)S(1)} %slice.197), channel_id=1, source_target_pairs={{0,1},{1,2},{2,3},{3,4},{4,5},{5,6},{6,7},{7,8},{8,9},{9,10},{10,1... | collective-permute-start | bytes 393224 | tf_op jit(solution)/shard_map/ppermute | solution.py:22
  230.7 7.6 %collective-permute-start.3 = (bf16[32,4,1,512]{3,0,2,1:T(8,128)(2,1)S(1)}, bf16[32,4,1,512]{3,0,2,1:T(8,128)(2,1)S(1)}, u32[]{:S(2)}, u32[]{:S(2)}) collective-permute-start(bf16[32,4,1,512]{3,0,2,1:T(8,128)(2,1)S(1)} %slice.196), channel_id=1, source_target_pairs={{1,0},{2,1},{3,2},{4,3},{5,4},{6,5},{7,6},{8,7},{9,8},{10,9},{11,1... | collective-permute-start | bytes 393224 | tf_op jit(solution)/shard_map/ppermute | solution.py:22
  244.2 8.4 %collective-permute-start.4 = (bf16[32,4,1,512]{3,0,2,1:T(8,128)(2,1)S(1)}, bf16[32,4,1,512]{3,0,2,1:T(8,128)(2,1)S(1)}, u32[]{:S(2)}, u32[]{:S(2)}) collective-permute-start(bf16[32,4,1,512]{3,0,2,1:T(8,128)(2,1)S(1)} %slice.195), channel_id=1, source_target_pairs={{0,1},{1,2},{2,3},{3,4},{4,5},{5,6},{6,7},{7,8},{8,9},{9,10},{10,1... | collective-permute-start | bytes 393224 | tf_op jit(solution)/shard_map/ppermute | solution.py:22
  257.9 7.6 %collective-permute-start.5 = (bf16[32,4,1,512]{3,0,2,1:T(8,128)(2,1)S(1)}, bf16[32,4,1,512]{3,0,2,1:T(8,128)(2,1)S(1)}, u32[]{:S(2)}, u32[]{:S(2)}) collective-permute-start(bf16[32,4,1,512]{3,0,2,1:T(8,128)(2,1)S(1)} %slice.194), channel_id=1, source_target_pairs={{1,0},{2,1},{3,2},{4,3},{5,4},{6,5},{7,6},{8,7},{9,8},{10,9},{11,1... | collective-permute-start | bytes 393224 | tf_op jit(solution)/shard_map/ppermute | solution.py:22
  271.4 8.4 %collective-permute-start.6 = (bf16[32,4,1,512]{3,0,2,1:T(8,128)(2,1)S(1)}, bf16[32,4,1,512]{3,0,2,1:T(8,128)(2,1)S(1)}, u32[]{:S(2)}, u32[]{:S(2)}) collective-permute-start(bf16[32,4,1,512]{3,0,2,1:T(8,128)(2,1)S(1)} %slice.193), channel_id=1, source_target_pairs={{0,1},{1,2},{2,3},{3,4},{4,5},{5,6},{6,7},{7,8},{8,9},{9,10},{10,1... | collective-permute-start | bytes 393224 | tf_op jit(solution)/shard_map/ppermute | solution.py:22
  285.1 7.8 %collective-permute-start.7 = (bf16[32,4,1,512]{3,0,2,1:T(8,128)(2,1)S(1)}, bf16[32,4,1,512]{3,0,2,1:T(8,128)(2,1)S(1)}, u32[]{:S(2)}, u32[]{:S(2)}) collective-permute-start(bf16[32,4,1,512]{3,0,2,1:T(8,128)(2,1)S(1)} %slice.192), channel_id=1, source_target_pairs={{1,0},{2,1},{3,2},{4,3},{5,4},{6,5},{7,6},{8,7},{9,8},{10,9},{11,1... | collective-permute-start | bytes 393224 | tf_op jit(solution)/shard_map/ppermute | solution.py:22
  298.8 8.4 %collective-permute-start.8 = (bf16[32,4,1,512]{3,0,2,1:T(8,128)(2,1)S(1)}, bf16[32,4,1,512]{3,0,2,1:T(8,128)(2,1)S(1)}, u32[]{:S(2)}, u32[]{:S(2)}) collective-permute-start(bf16[32,4,1,512]{3,0,2,1:T(8,128)(2,1)S(1)} %slice.191), channel_id=1, source_target_pairs={{0,1},{1,2},{2,3},{3,4},{4,5},{5,6},{6,7},{7,8},{8,9},{9,10},{10,1... | collective-permute-start | bytes 393224 | tf_op jit(solution)/shard_map/ppermute | solution.py:22
  312.5 7.6 %collective-permute-start.9 = (bf16[32,4,1,512]{3,0,2,1:T(8,128)(2,1)S(1)}, bf16[32,4,1,512]{3,0,2,1:T(8,128)(2,1)S(1)}, u32[]{:S(2)}, u32[]{:S(2)}) collective-permute-start(bf16[32,4,1,512]{3,0,2,1:T(8,128)(2,1)S(1)} %slice.190), channel_id=1, source_target_pairs={{1,0},{2,1},{3,2},{4,3},{5,4},{6,5},{7,6},{8,7},{9,8},{10,9},{11,1... | collective-permute-start | bytes 393224 | tf_op jit(solution)/shard_map/ppermute | solution.py:22
  326.0 8.4 %collective-permute-start.10 = (bf16[32,4,1,512]{3,0,2,1:T(8,128)(2,1)S(1)}, bf16[32,4,1,512]{3,0,2,1:T(8,128)(2,1)S(1)}, u32[]{:S(2)}, u32[]{:S(2)}) collective-permute-start(bf16[32,4,1,512]{3,0,2,1:T(8,128)(2,1)S(1)} %slice.189), channel_id=1, source_target_pairs={{0,1},{1,2},{2,3},{3,4},{4,5},{5,6},{6,7},{7,8},{8,9},{9,10},{10,1... | collective-permute-start | bytes 393224 | tf_op jit(solution)/shard_map/ppermute | solution.py:22
  334.5 7.6 %copy-start.1 = (f32[128,64]{0,1:T(8,128)S(1)}, f32[128,64]{0,1:T(8,128)}, u32[]{:S(2)}) copy-start(f32[128,64]{0,1:T(8,128)} %param.11) | copy-start | bytes 98308
Sparse Core Ops, SparseCore 0:
  15.0 85.3 all-gather.2
